TPU v7x, 32 devices: a whole 2x2x4 slice. The times are simulated.
32 devices in a mesh: dp: 4 (over y, x), item: 8 (over z, core).
Axes of the slice: x: 2, y: 2, z: 4, core: 2. Of those that a mesh axis runs over, the one named last changes fastest.
Arguments:
- queries: bfloat16 [32768, 256], P(('dp', 'item')), may hold values from -0.5 to 0.5
- item_table: float32 [32768, 256], P('item'), may hold values from -0.5 to 0.5
- adagrad_state: float32 [32768], P('item'), may hold values from 1 to 1000
- pos_owner: int32 [32768, 1], P(('dp', 'item')), may hold values from 0 to 7; in each aligned block of 1024 rows (0 to 1023, 1024 to 2047, ...) at most 384 rows name the same one
- pos_row: int32 [32768], P(('dp', 'item')), may hold values from 0 to 4095
- neg_rows: int32 [1536], P(('dp', 'item')), may hold values from 0 to 4095
Outputs:
- query_grad: bfloat16 [32768, 256], P(('dp', 'item'))
- example_loss: float32 [32768], P(('dp', 'item'))
- new_table: float32 [32768, 256], P('item')
- new_state: float32 [32768], P('item')
Inputs may be any that keep to these rules, and one draw needn't show every extreme that they name: `pos_owner`: within the rows of one device (aligned blocks of 1024 examples) no shard is named more than 384 times; some device's block names one shard exactly 384 times.
All inputs are finite; a program needn't handle non-finite values.
Results may differ from a plain program's by a relative error of at most 0.0049.
Values may be sent and summed in bfloat16 or wider, within the bound.
No kernel may reach another device: no remote copies, remote signals or barrier semaphores. Data moves between devices by JAX's collectives and lax.ppermute only.
A program may use at most 64 MiB of HBM per device.

v0:
```python
import math
import jax
import jax.numpy as jnp
from jax import lax
from jax.sharding import PartitionSpec as P

INV_TEMP = 20.0
LEARN_RATE = 0.05
EPSILON = 1e-06


def unit_rows(matrix):
    row_norm = jnp.sqrt(jnp.sum(matrix * matrix, axis=-1, keepdims=True) + EPSILON)
    return (matrix / row_norm, row_norm)


def on_device(queries, item_table, adagrad_state, pos_owner, pos_row, neg_rows):
    ex_count = queries.shape[0]
    rows_dev = item_table.shape[0]
    feat_width = item_table.shape[1]
    neg_dev = neg_rows.shape[0]
    item_count = lax.axis_size("item")
    dp_count = lax.axis_size("dp")
    capacity = 3 * ex_count // item_count
    item_index = lax.axis_index("item")
    query_hat, query_norm = unit_rows(queries.astype(jnp.float32))
    query_send = query_hat.astype(jnp.bfloat16)
    unit_table, table_norm = unit_rows(item_table)
    table_send = unit_table.astype(jnp.bfloat16)
    owners = pos_owner[:, 0]
    onehot = (owners[:, None] == jnp.arange(item_count, dtype=jnp.int32)[None, :]).astype(jnp.int32)
    earlier = jnp.cumsum(onehot, axis=0) - onehot
    slots = jnp.sum(earlier * onehot, axis=1)
    places = owners * capacity + slots
    requests = jnp.zeros((item_count * capacity,), jnp.int32).at[places].set(pos_row)
    requests = requests.reshape(item_count, capacity)
    asked_rows = lax.all_to_all(requests, "item", split_axis=0, concat_axis=0, tiled=True)
    found = table_send[asked_rows]
    returned = lax.all_to_all(found, "item", split_axis=0, concat_axis=0, tiled=True)
    pos_e = returned.reshape(item_count * capacity, feat_width)[places]
    pos_gid = owners * rows_dev + pos_row
    my_gid = item_index * rows_dev + neg_rows
    my_neg = table_send[neg_rows]
    block_rows, block_ids = (
        lax.all_gather(my_neg, "item", axis=0, tiled=True),
        lax.all_gather(my_gid, "item", axis=0, tiled=True),
    )
    all_rows, all_ids = (
        lax.all_gather(block_rows, "dp", axis=0, tiled=True),
        lax.all_gather(block_ids, "dp", axis=0, tiled=True),
    )
    negs = all_rows.shape[0]
    block_size = math.gcd(negs, 1024)
    block_count = negs // block_size
    row_blocks = all_rows.reshape(block_count, block_size, feat_width)
    id_blocks = all_ids.reshape(block_count, block_size)

    def block_scores(row_block, id_block):
        scores = (
            jnp.einsum("ed,nd->en", query_send, row_block, preferred_element_type=jnp.float32)
            * INV_TEMP
        )
        allowed = id_block[None, :] != pos_gid[:, None]
        return (scores, allowed)

    s_pos = INV_TEMP * jnp.sum(query_send.astype(jnp.float32) * pos_e.astype(jnp.float32), axis=1)

    def add_exp(carry, pieces):
        scores, allowed = block_scores(pieces[0], pieces[1])
        return (carry + jnp.sum(jnp.where(allowed, jnp.exp(scores), 0.0), axis=1), None)

    neg_totals, _ = lax.scan(add_exp, jnp.zeros((ex_count,), jnp.float32), (row_blocks, id_blocks))
    lse = jnp.log(jnp.exp(s_pos) + neg_totals)
    example_loss = lse - s_pos

    def both_products(carry, pieces):
        scores, allowed = block_scores(pieces[0], pieces[1])
        probs = jnp.where(allowed, jnp.exp(scores - lse[:, None]), 0.0).astype(jnp.bfloat16)
        carry = carry + jnp.dot(probs, pieces[0], preferred_element_type=jnp.float32)
        partial_rows = INV_TEMP * jnp.einsum(
            "en,ed->nd", probs, query_send, preferred_element_type=jnp.float32
        )
        return (carry, partial_rows)

    neg_part, partial_blocks = lax.scan(
        both_products, jnp.zeros((ex_count, feat_width), jnp.float32), (row_blocks, id_blocks)
    )
    neg_partials = partial_blocks.reshape(negs, feat_width)
    p_pos = jnp.exp(s_pos - lse)
    g_query = INV_TEMP * ((p_pos - 1.0)[:, None] * pos_e.astype(jnp.float32) + neg_part)
    query_grad = (
        (g_query - query_hat * jnp.sum(query_hat * g_query, axis=1, keepdims=True)) / query_norm
    ).astype(jnp.bfloat16)
    g_pos = INV_TEMP * (p_pos - 1.0)[:, None] * query_hat
    outbox = jnp.zeros((item_count * capacity, feat_width), jnp.float32).at[places].set(g_pos)
    outbox = outbox.reshape(item_count, capacity, feat_width)
    inbox = lax.all_to_all(
        outbox.astype(jnp.bfloat16), "item", split_axis=0, concat_axis=0, tiled=True
    ).astype(outbox.dtype)
    dense = jnp.zeros((rows_dev, feat_width), jnp.float32)
    dense = dense.at[asked_rows.reshape(-1)].add(inbox.reshape(-1, feat_width))
    item_partials = (
        neg_partials.reshape(dp_count, item_count, neg_dev, feat_width)
        .transpose(1, 0, 2, 3)
        .reshape(negs, feat_width)
    )
    item_ids = all_ids.reshape(dp_count, item_count, neg_dev).transpose(1, 0, 2).reshape(negs)
    span_rows = dp_count * neg_dev
    neg_grad = lax.psum_scatter(
        item_partials.astype(jnp.bfloat16), "item", scatter_dimension=0, tiled=True
    ).astype(jnp.float32)
    local_rows = (
        lax.dynamic_slice_in_dim(item_ids, item_index * span_rows, span_rows, 0)
        - item_index * rows_dev
    )
    dense = dense.at[local_rows].add(neg_grad)
    g_unit = lax.psum(dense.astype(jnp.bfloat16), "dp").astype(jnp.float32)
    g_row = (g_unit - unit_table * jnp.sum(unit_table * g_unit, axis=1, keepdims=True)) / table_norm
    new_state = adagrad_state + jnp.mean(g_row * g_row, axis=1)
    new_table = item_table - LEARN_RATE * g_row / jnp.sqrt(new_state)[:, None]
    return (query_grad, example_loss, new_table, new_state)


def solution(mesh):
    placed = (
        P(("dp", "item"), None),
        P("item", None),
        P("item"),
        P(("dp", "item"), None),
        P(("dp", "item")),
        P(("dp", "item")),
    )
    return jax.shard_map(
        on_device,
        mesh=mesh,
        in_specs=placed,
        out_specs=(P(("dp", "item"), None), P(("dp", "item")), P("item", None), P("item")),
        check_vma=False,
    )
```

profile of v0, /device:TPU:0, one launch (start us, length us, event | category | flops | bytes accessed | tf_op | source)
XLA Modules:
  0.0 306.5 jit_solution(16396751657277209719)
XLA Ops:
  7.9 2.3 reduce-window.6
  12.1 5.0 %scatter_custom_fusion = s32[3072]{0:T(1024)} fusion(s32[1024]{0:T(1024)S(1)} %bitcast.110, s32[1024]{0:T(1024)} %param.14, s32[]{:T(128)} %constant.35.clone.1), kind=kCustom, calls=%fused_computation.69 | custom fusion | bytes 12800 | tf_op jit(solution)/shard_map/scatter | solution.py:35
  17.1 6.4 %all-to-all-start = ((s32[8,1,384]{2,1,0:T(1,128)}), s32[8,1,384]{2,1,0:T(1,128)S(1)}, u32[]{:S(2)}, u32[]{:S(2)}) async-start(s32[8,1,384]{2,1,0:T(1,128)} %bitcast.5), calls=%async_computation | async-start | bytes 24576 | tf_op jit(solution)/shard_map/all_to_all | solution.py:37
  23.5 3.0 multiply_reduce_fusion.1
  29.1 13.0 %gather_fusion = bf16[3072,256]{1,0:T(8,128)(2,1)} fusion(bf16[4096,256]{1,0:T(8,128)(2,1)S(1)} %fusion.35, s32[3072]{0:T(1024)S(1)} %broadcast_clamp_fusion), kind=kCustom, calls=%fused_computation | custom fusion | bytes 3158016 | tf_op jit(solution)/shard_map/gather | solution.py:38
  42.2 4.4 %all-to-all-start.1 = ((bf16[8,384,256]{2,1,0:T(8,128)(2,1)}), bf16[8,384,256]{2,1,0:T(8,128)(2,1)}, u32[]{:S(2)}, u32[]{:S(2)}) async-start(bf16[8,384,256]{2,1,0:T(8,128)(2,1)} %bitcast.96), calls=%async_computation.1 | async-start | bytes 3145728 | tf_op jit(solution)/shard_map/all_to_all | solution.py:39
  48.0 36.5 %all-reduce = s32[384]{0:T(512)S(1)} all-reduce(s32[384]{0:T(512)S(1)} %get-tuple-element.167), channel_id=1, replica_groups=mesh['dp'=4,'item'=8] {'item'}, use_global_device_ids=true, to_apply=%add | all-reduce | flops 384 | bytes 3072
  84.6 8.1 %all-gather.2 = s32[4,1,384]{2,1,0:T(1,128)S(1)} all-gather(s32[1,1,384]{2,1,0:T(1,128)S(1)} %reshape.211), channel_id=1, replica_groups=mesh['dp'=4,'item'=8] {'dp'}, dimensions={0}, use_global_device_ids=true | all-gather | bytes 7680 | tf_op jit(solution)/shard_map/all_gather | solution.py:50
  93.4 14.1 %all-gather = bf16[384,256]{1,0:T(8,128)(2,1)S(1)} all-gather(bf16[48,256]{1,0:T(8,128)(2,1)S(1)} %gather_fusion.2), channel_id=2, replica_groups=mesh['dp'=4,'item'=8] {'item'}, dimensions={0}, use_global_device_ids=true | all-gather | bytes 221184 | tf_op jit(solution)/shard_map/all_gather | solution.py:45
  108.8 12.4 %all-gather.1 = bf16[1536,256]{1,0:T(8,128)(2,1)S(1)} all-gather(bf16[384,256]{1,0:T(8,128)(2,1)S(1)} %all-gather), channel_id=3, replica_groups=mesh['dp'=4,'item'=8] {'dp'}, dimensions={0}, use_global_device_ids=true | all-gather | bytes 983040 | tf_op jit(solution)/shard_map/all_gather | solution.py:49
  121.2 5.1 %gather_fusion.1 = bf16[1024,256]{1,0:T(8,128)(2,1)S(1)} fusion(bf16[3072,256]{1,0:T(8,128)(2,1)} %bitcast.9, s32[1024]{0:T(1024)S(1)} %broadcast_clamp_fusion.1), kind=kCustom, calls=%fused_computation.1 | custom fusion | bytes 1052672 | tf_op jit(solution)/shard_map/gather | solution.py:40
  126.8 2.0 while.24
  129.4 7.1 %scatter_custom_fusion.1 = f32[3072,256]{1,0:T(8,128)} fusion(s32[1024]{0:T(1024)S(1)} %bitcast.112, f32[]{:T(128)} %constant.11.clone.1, f32[1024]{0:T(1024)S(1)} %get-tuple-element.160, bf16[1024,256]{1,0:T(8,128)(2,1)S(1)} %copy-done.3, f32[1024]{0:T(1024)S(1)} %add_sqrt_fusion.1), kind=kCustom, calls=%fused_computation.38 | custom fusion | flops 786432 | bytes 3678212 | tf_op jit(solution)/shard_map/scatter | solution.py:95
  136.5 3.2 %convert_element_type.65 = bf16[3072,256]{1,0:T(8,128)(2,1)} convert(f32[3072,256]{1,0:T(8,128)} %scatter_custom_fusion.1) | non-fusion elementwise | flops 786432 | bytes 4718592 | tf_op jit(solution)/shard_map/convert_element_type | solution.py:98
  139.7 4.3 %all-to-all-start.2 = ((bf16[8,384,256]{2,1,0:T(8,128)(2,1)}), bf16[8,384,256]{2,1,0:T(8,128)(2,1)}, u32[]{:S(2)}, u32[]{:S(2)}) async-start(bf16[8,384,256]{2,1,0:T(8,128)(2,1)} %bitcast.97), calls=%async_computation.2 | async-start | bytes 3145728 | tf_op jit(solution)/shard_map/all_to_all | solution.py:97
  144.1 7.4 %while.25 = (s32[]{:T(128)}, f32[1024,256]{1,0:T(8,128)S(1)}, bf16[3,512,256]{2,1,0:T(8,128)(2,1)}, s32[3,512]{1,0:T(4,128)S(1)}, s32[1024]{0:T(1024)S(1)}, /*in...) while((s32[]{:T(128)}, f32[1024,256]{1,0:T(8,128)S(1)}, ...), condition=%wide.region_11.12_spmd.clone, body=%wide.region_10.11_spmd.clone.sunk | while | flops 808583168 | bytes 13646015 | solution.py:85
  151.5 2.1 copy.15
  154.1 34.6 %all-to-all-done.2 = bf16[8,384,256]{2,1,0:T(8,128)(2,1)} async-done(((bf16[8,384,256]{2,1,0:T(8,128)(2,1)}), bf16[8,384,256]{2,1,0:T(8,128)(2,1)}, u32[]{:S(2)}, u32[]{:S(2)}) %all-to-all-start.2) | async-done | bytes 1572896 | tf_op jit(solution)/shard_map/all_to_all | solution.py:97
  188.7 22.8 %scatter_custom_fusion.2 = f32[4096,256]{1,0:T(8,128)} fusion(s32[3072]{0:T(1024)S(1)} %bitcast.114, bf16[3072,256]{1,0:T(8,128)(2,1)} %bitcast.27, f32[]{:T(128)} %constant.11.clone.1), kind=kCustom, calls=%fused_computation.34 | custom fusion | flops 1572864 | bytes 5767172 | tf_op jit(solution)/shard_map/scatter-add | solution.py:101
  211.4 6.0 %scatter_custom_fusion.3 = f32[4096,256]{1,0:T(8,128)} fusion(f32[4096,256]{1,0:T(8,128)} %scatter_custom_fusion.2, s32[192]{0:T(256)S(1)} %compare_select_fusion.3, bf16[192,256]{1,0:T(8,128)(2,1)} %reduce-scatter.2.cloned.1.call-done), kind=kCustom, calls=%fused_computation.52 | custom fusion | flops 98304 | bytes 4292608 | tf_op jit(solution)/shard_map/scatter-add | solution.py:116
  217.5 3.7 %convert_element_type.72 = bf16[4096,256]{1,0:T(8,128)(2,1)} convert(f32[4096,256]{1,0:T(8,128)} %scatter_custom_fusion.3) | non-fusion elementwise | flops 1048576 | bytes 6291456 | tf_op jit(solution)/shard_map/convert_element_type | solution.py:117
  223.0 64.8 %all-reduce.3.cloned.1.call-done = bf16[4096,256]{1,0:T(8,128)(2,1)} async-done(((bf16[4096,256]{1,0:T(8,128)(2,1)}), bf16[4096,256]{1,0:T(8,128)(2,1)}) %all-reduce.3.cloned.1.call-update) | async-done | bytes 2097168 | tf_op jit(solution)/shard_map/psum | solution.py:117
  287.8 3.9 %fusion.13 = f32[4096]{0:T(1024)S(1)} fusion(bf16[4096,256]{1,0:T(8,128)(2,1)} %all-reduce.3.cloned.1.call-done, f32[4096,256]{1,0:T(8,128)} %param.11, f32[4096]{0:T(1024)S(1)} %add_sqrt_fusion), kind=kLoop, calls=%fused_computation.29 | loop fusion | flops 4190208 | bytes 6324224 | tf_op jit(solution)/shard_map/reduce_sum | solution.py:118
  295.1 4.5 %divide_subtract_fusion = f32[4096,256]{1,0:T(8,128)} fusion(f32[4096,256]{1,0:T(8,128)S(1)} %copy-done.1, f32[4096]{0:T(1024)S(1)} %get-tuple-element.158, f32[4096]{0:T(1024)S(1)} %add_sqrt_fusion, f32[4096]{0:T(1024)S(1)} %fusion.13, bf16[4096,256]{1,0:T(8,128)(2,1)S(1)} %copy-done.2), kind=kLoop, calls=%fused_computation.31 | loop fusion | flops 8388608 | bytes 10534912 | tf_op jit(solution)/shard_map/sub | solution.py:120
  (94 shorter events, 24.1 us)
Async XLA Ops:
  17.1 12.0 %all-to-all-start = ((s32[8,1,384]{2,1,0:T(1,128)}), s32[8,1,384]{2,1,0:T(1,128)S(1)}, u32[]{:S(2)}, u32[]{:S(2)}) async-start(s32[8,1,384]{2,1,0:T(1,128)} %bitcast.5), calls=%async_computation | async-start | bytes 24576 | tf_op jit(solution)/shard_map/all_to_all | solution.py:37
  23.5 3.4 %copy-start = (f32[4096,256]{1,0:T(8,128)S(1)}, f32[4096,256]{1,0:T(8,128)}, u32[]{:S(2)}) copy-start(f32[4096,256]{1,0:T(8,128)} %param.11) | copy-start | bytes 12582916
  42.2 4.5 %copy-start.10 = (u32[32]{0:T(128)S(1)}, u32[32]{0:T(128)}, u32[]{:S(2)}) copy-start(u32[32]{0:T(128)} %constant.31) | copy-start | bytes 388
  42.2 5.8 %copy-start.9 = (s32[48]{0:T(128)S(1)}, s32[48]{0:T(128)}, u32[]{:S(2)}) copy-start(s32[48]{0:T(128)} %param.15) | copy-start | bytes 580
  42.2 79.0 %copy-start.6 = (s32[1024,1]{0,1:T(1,128)S(1)}, s32[1024,1]{0,1:T(1,128)}, u32[]{:S(2)}) copy-start(s32[1024,1]{0,1:T(1,128)} %param.13) | copy-start | bytes 12292
  42.2 79.0 %copy-start.8 = (s32[1024]{0:T(1024)S(1)}, s32[1024]{0:T(1024)}, u32[]{:S(2)}) copy-start(s32[1024]{0:T(1024)} %param.14) | copy-start | bytes 12292
  42.2 79.1 %all-to-all-start.1 = ((bf16[8,384,256]{2,1,0:T(8,128)(2,1)}), bf16[8,384,256]{2,1,0:T(8,128)(2,1)}, u32[]{:S(2)}, u32[]{:S(2)}) async-start(bf16[8,384,256]{2,1,0:T(8,128)(2,1)} %bitcast.96), calls=%async_computation.1 | async-start | bytes 3145728 | tf_op jit(solution)/shard_map/all_to_all | solution.py:39
  107.5 18.9 %copy-start.3 = (bf16[1024,256]{1,0:T(8,128)(2,1)S(1)}, bf16[1024,256]{1,0:T(8,128)(2,1)}, u32[]{:S(2)}) copy-start(bf16[1024,256]{1,0:T(8,128)(2,1)} %param.10) | copy-start | bytes 1572868
  139.7 48.9 %all-to-all-start.2 = ((bf16[8,384,256]{2,1,0:T(8,128)(2,1)}), bf16[8,384,256]{2,1,0:T(8,128)(2,1)}, u32[]{:S(2)}, u32[]{:S(2)}) async-start(bf16[8,384,256]{2,1,0:T(8,128)(2,1)} %bitcast.97), calls=%async_computation.2 | async-start | bytes 3145728 | tf_op jit(solution)/shard_map/all_to_all | solution.py:97
  144.0 67.4 %reduce-scatter.2.cloned.1.call-start = ((), (), s32[]{:S(2)}) async-start(), calls=%async_computation.4 | async-start | bytes 884736 | tf_op jit(solution)/shard_map/reduce_scatter | solution.py:109
  144.1 1.1 copy-start.4
  145.7 0.9 copy-start.5
  146.6 1.1 copy-start.4
  148.1 0.9 copy-start.5
  149.0 1.1 copy-start.4
  150.6 0.9 copy-start.5
  153.6 134.2 %all-reduce.3.cloned.1.call-start = ((), (), s32[]{:S(2)}) async-start(), calls=%async_computation.5 | async-start | bytes 4194304 | tf_op jit(solution)/shard_map/psum | solution.py:117
  287.8 4.1 %copy-start.1 = (f32[4096,256]{1,0:T(8,128)S(1)}, f32[4096,256]{1,0:T(8,128)}, u32[]{:S(2)}) copy-start(f32[4096,256]{1,0:T(8,128)} %param.11) | copy-start | bytes 12582916
  287.8 4.7 %copy-start.2 = (bf16[4096,256]{1,0:T(8,128)(2,1)S(1)}, bf16[4096,256]{1,0:T(8,128)(2,1)}, u32[]{:S(2)}) copy-start(bf16[4096,256]{1,0:T(8,128)(2,1)} %all-reduce.3.cloned.1.call-done) | copy-start | bytes 6291460
  292.5 2.0 copy-start.7
Sparse Core Ops, SparseCore 0:
  153.7 36.1 reduce-scatter.1
  221.3 66.4 all-reduce.2
where the time goes:
time: 307 us
  waiting for transfers between devices  101 us (33%)
  blocking collectives  71.1 us (23%)
  other arithmetic  66.5 us (22%)
  local copies, waits for them, and re-layouts  29.8 us (10%)
  starting transfers between devices  15.3 us (5%)
  between operations  15 us (5%)
  matrix products  7.68 us (3%)
    psum x1, waiting for transfers between devices, on_device(): g_unit = lax.psum(dense.astype(jnp.bfloat16), 'dp').astype(jnp.float32)  64.8 us
    unnamed x1, blocking collectives  36.5 us
    all_to_all x1, waiting for transfers between devices, on_device(): lax.all_to_all(outbox.astype(jnp.bfloat16), 'item', split_axis=0, concat_...  34.6 us
    scatter-add x1, other arithmetic, on_device(): dense = dense.at[asked_rows.reshape(-1)].add(inbox.reshape(-1, feat_width))  22.8 us
    all_gather x1, blocking collectives, on_device(): lax.all_gather(my_neg, 'item', axis=0, tiled=True)  14.1 us
    gather x1, local copies, waits for them, and re-layouts, on_device(): found = table_send[asked_rows]  13 us
    all_gather x1, blocking collectives, on_device(): lax.all_gather(block_rows, 'dp', axis=0, tiled=True)  12.4 us
    all_gather x1, blocking collectives, on_device(): lax.all_gather(block_ids, 'dp', axis=0, tiled=True)  8.08 us
  transfers between devices with their start and end apart: 5, of which 3 were waited for; matrix products, arithmetic and copies ran while one was open for 13% of the time, Pallas kernels for 0%

commit v1 on v0

--- a/solution.py
+++ b/solution.py
@@ -114,7 +114,7 @@
         - item_index * rows_dev
     )
     dense = dense.at[local_rows].add(neg_grad)
-    g_unit = lax.psum(dense.astype(jnp.bfloat16), "dp").astype(jnp.float32)
+    g_unit = jnp.sum(lax.all_gather(dense.astype(jnp.bfloat16), "dp"), axis=0).astype(jnp.float32)
     g_row = (g_unit - unit_table * jnp.sum(unit_table * g_unit, axis=1, keepdims=True)) / table_norm
     new_state = adagrad_state + jnp.mean(g_row * g_row, axis=1)
     new_table = item_table - LEARN_RATE * g_row / jnp.sqrt(new_state)[:, None]

time: 307 us -> 330 us (1.075)
  waiting for transfers between devices: 101 us -> 119 us
  other arithmetic: 66.5 us -> 72 us
    all_gather x0 -> x1, waiting for transfers between devices: none -> 82.8 us  [on_device(): lax.all_gather(dense.astype(jnp.bfloat16), 'dp')]
    psum x1 -> x0, waiting for transfers between devices: 64.8 us -> none  [on_device(): g_unit = lax.psum(dense.astype(jnp.bfloat16), 'dp').astype(jnp.float32)]
    reduce_sum x0 -> x1, other arithmetic: none -> 6.04 us  [on_device(): jnp.sum(lax.all_gather(dense.astype(jnp.bfloat16), 'dp'), axis=0)]
  transfers between devices with their start and end apart: 5 -> 5, of which waited for: 3 -> 3; matrix products, arithmetic and copies ran while one was open for 13% -> 12% of each run, Pallas kernels for 0% -> 0%
where the time goes in v1:
time: 330 us; the launch traced here: 329 us
  waiting for transfers between devices  119 us (36%)
  other arithmetic  72 us (22%)
  blocking collectives  71.1 us (22%)
  local copies, waits for them, and re-layouts  29.2 us (9%)
  starting transfers between devices  15.3 us (5%)
  between operations  15 us (5%)
  matrix products  7.68 us (2%)
    all_gather x1, waiting for transfers between devices, on_device(): lax.all_gather(dense.astype(jnp.bfloat16), 'dp')  82.8 us
    unnamed x1, blocking collectives  36.5 us
    all_to_all x1, waiting for transfers between devices, on_device(): lax.all_to_all(outbox.astype(jnp.bfloat16), 'item', split_axis=0, concat_...  34.6 us
    scatter-add x1, other arithmetic, on_device(): dense = dense.at[asked_rows.reshape(-1)].add(inbox.reshape(-1, feat_width))  22.8 us
    all_gather x1, blocking collectives, on_device(): lax.all_gather(my_neg, 'item', axis=0, tiled=True)  14.1 us
    gather x1, local copies, waits for them, and re-layouts, on_device(): found = table_send[asked_rows]  13 us
    all_gather x1, blocking collectives, on_device(): lax.all_gather(block_rows, 'dp', axis=0, tiled=True)  12.4 us
    all_gather x1, blocking collectives, on_device(): lax.all_gather(block_ids, 'dp', axis=0, tiled=True)  8.08 us
  transfers between devices with their start and end apart: 5, of which 3 were waited for; matrix products, arithmetic and copies ran while one was open for 12% of the time, Pallas kernels for 0%

profile of v1, /device:TPU:0, one launch (start us, length us, event | category | flops | bytes accessed | tf_op | source)
XLA Modules:
  0.0 329.4 jit_solution(16113619109597088170)
XLA Ops:
  7.9 2.3 reduce-window.6
  12.1 5.0 %scatter_custom_fusion = s32[3072]{0:T(1024)} fusion(s32[1024]{0:T(1024)S(1)} %bitcast.112, s32[1024]{0:T(1024)} %param.14, s32[]{:T(128)} %constant.36.clone.1), kind=kCustom, calls=%fused_computation.69 | custom fusion | bytes 12800 | tf_op jit(solution)/shard_map/scatter | solution.py:35
  17.1 6.4 %all-to-all-start = ((s32[8,1,384]{2,1,0:T(1,128)}), s32[8,1,384]{2,1,0:T(1,128)S(1)}, u32[]{:S(2)}, u32[]{:S(2)}) async-start(s32[8,1,384]{2,1,0:T(1,128)} %bitcast.5), calls=%async_computation | async-start | bytes 24576 | tf_op jit(solution)/shard_map/all_to_all | solution.py:37
  23.5 3.0 multiply_reduce_fusion.1
  29.1 13.0 %gather_fusion = bf16[3072,256]{1,0:T(8,128)(2,1)} fusion(bf16[4096,256]{1,0:T(8,128)(2,1)S(1)} %fusion.35, s32[3072]{0:T(1024)S(1)} %broadcast_clamp_fusion), kind=kCustom, calls=%fused_computation | custom fusion | bytes 3158016 | tf_op jit(solution)/shard_map/gather | solution.py:38
  42.2 4.4 %all-to-all-start.1 = ((bf16[8,384,256]{2,1,0:T(8,128)(2,1)}), bf16[8,384,256]{2,1,0:T(8,128)(2,1)}, u32[]{:S(2)}, u32[]{:S(2)}) async-start(bf16[8,384,256]{2,1,0:T(8,128)(2,1)} %bitcast.98), calls=%async_computation.1 | async-start | bytes 3145728 | tf_op jit(solution)/shard_map/all_to_all | solution.py:39
  48.0 36.5 %all-reduce = s32[384]{0:T(512)S(1)} all-reduce(s32[384]{0:T(512)S(1)} %get-tuple-element.167), channel_id=1, replica_groups=mesh['dp'=4,'item'=8] {'item'}, use_global_device_ids=true, to_apply=%add | all-reduce | flops 384 | bytes 3072
  84.6 8.1 %all-gather.3 = s32[4,1,384]{2,1,0:T(1,128)S(1)} all-gather(s32[1,1,384]{2,1,0:T(1,128)S(1)} %reshape.212), channel_id=1, replica_groups=mesh['dp'=4,'item'=8] {'dp'}, dimensions={0}, use_global_device_ids=true | all-gather | bytes 7680 | tf_op jit(solution)/shard_map/all_gather | solution.py:50
  93.4 14.1 %all-gather = bf16[384,256]{1,0:T(8,128)(2,1)S(1)} all-gather(bf16[48,256]{1,0:T(8,128)(2,1)S(1)} %gather_fusion.2), channel_id=2, replica_groups=mesh['dp'=4,'item'=8] {'item'}, dimensions={0}, use_global_device_ids=true | all-gather | bytes 221184 | tf_op jit(solution)/shard_map/all_gather | solution.py:45
  108.8 12.4 %all-gather.1 = bf16[1536,256]{1,0:T(8,128)(2,1)S(1)} all-gather(bf16[384,256]{1,0:T(8,128)(2,1)S(1)} %all-gather), channel_id=3, replica_groups=mesh['dp'=4,'item'=8] {'dp'}, dimensions={0}, use_global_device_ids=true | all-gather | bytes 983040 | tf_op jit(solution)/shard_map/all_gather | solution.py:49
  121.2 5.1 %gather_fusion.1 = bf16[1024,256]{1,0:T(8,128)(2,1)S(1)} fusion(bf16[3072,256]{1,0:T(8,128)(2,1)} %bitcast.9, s32[1024]{0:T(1024)S(1)} %broadcast_clamp_fusion.1), kind=kCustom, calls=%fused_computation.1 | custom fusion | bytes 1052672 | tf_op jit(solution)/shard_map/gather | solution.py:40
  129.4 7.1 %scatter_custom_fusion.1 = f32[3072,256]{1,0:T(8,128)} fusion(s32[1024]{0:T(1024)S(1)} %bitcast.114, f32[]{:T(128)} %constant.34.clone.1, f32[1024]{0:T(1024)S(1)} %get-tuple-element.160, bf16[1024,256]{1,0:T(8,128)(2,1)S(1)} %copy-done.2, f32[1024]{0:T(1024)S(1)} %add_sqrt_fusion.1), kind=kCustom, calls=%fused_computation.38 | custom fusion | flops 786432 | bytes 3678212 | tf_op jit(solution)/shard_map/scatter | solution.py:95
  136.5 3.2 convert_element_type.67
  139.7 4.3 %all-to-all-start.2 = ((bf16[8,384,256]{2,1,0:T(8,128)(2,1)}), bf16[8,384,256]{2,1,0:T(8,128)(2,1)}, u32[]{:S(2)}, u32[]{:S(2)}) async-start(bf16[8,384,256]{2,1,0:T(8,128)(2,1)} %bitcast.99), calls=%async_computation.2 | async-start | bytes 3145728 | tf_op jit(solution)/shard_map/all_to_all | solution.py:97
  144.1 7.4 %while.25 = (s32[]{:T(128)}, f32[1024,256]{1,0:T(8,128)S(1)}, bf16[3,512,256]{2,1,0:T(8,128)(2,1)}, s32[3,512]{1,0:T(4,128)S(1)}, s32[1024]{0:T(1024)S(1)}, /*in...) while((s32[]{:T(128)}, f32[1024,256]{1,0:T(8,128)S(1)}, ...), condition=%wide.region_11.12_spmd.clone, body=%wide.region_10.11_spmd.clone.sunk | while | flops 808583168 | bytes 13646015 | solution.py:85
  151.5 2.1 copy.15
  154.1 34.6 %all-to-all-done.2 = bf16[8,384,256]{2,1,0:T(8,128)(2,1)} async-done(((bf16[8,384,256]{2,1,0:T(8,128)(2,1)}), bf16[8,384,256]{2,1,0:T(8,128)(2,1)}, u32[]{:S(2)}, u32[]{:S(2)}) %all-to-all-start.2) | async-done | bytes 1572896 | tf_op jit(solution)/shard_map/all_to_all | solution.py:97
  188.7 22.8 %scatter_custom_fusion.2 = f32[4096,256]{1,0:T(8,128)} fusion(s32[3072]{0:T(1024)S(1)} %bitcast.116, bf16[3072,256]{1,0:T(8,128)(2,1)} %bitcast.28, f32[]{:T(128)} %constant.34.clone.1), kind=kCustom, calls=%fused_computation.34 | custom fusion | flops 1572864 | bytes 5767172 | tf_op jit(solution)/shard_map/scatter-add | solution.py:101
  211.4 6.0 %scatter_custom_fusion.3 = f32[4096,256]{1,0:T(8,128)} fusion(f32[4096,256]{1,0:T(8,128)} %scatter_custom_fusion.2, s32[192]{0:T(256)S(1)} %compare_select_fusion.3, bf16[192,256]{1,0:T(8,128)(2,1)} %reduce-scatter.2.cloned.1.call-done), kind=kCustom, calls=%fused_computation.52 | custom fusion | flops 98304 | bytes 4292608 | tf_op jit(solution)/shard_map/scatter-add | solution.py:116
  217.5 3.8 %convert_element_type.74 = bf16[4096,256]{1,0:T(8,128)(2,1)} convert(f32[4096,256]{1,0:T(8,128)} %scatter_custom_fusion.3) | non-fusion elementwise | flops 1048576 | bytes 6291456 | tf_op jit(solution)/shard_map/convert_element_type | solution.py:117
  223.1 82.8 %all-gather.6.cloned.1.call-done = bf16[16384,256]{1,0:T(8,128)(2,1)} async-done(((bf16[4096,256]{1,0:T(8,128)(2,1)}), bf16[16384,256]{1,0:T(8,128)(2,1)}) %all-gather.6.cloned.1.call-update) | async-done | bytes 8388624 | tf_op jit(solution)/shard_map/all_gather | solution.py:117
  305.9 6.0 %reduce_sum.92 = bf16[4096,256]{1,0:T(8,128)(2,1)S(1)} reduce(bf16[4,4096,256]{2,1,0:T(8,128)(2,1)} %bitcast.97, bf16[]{:T(256)} %constant.22.clone.1), dimensions={0}, to_apply=%region_17.18 | reduce | flops 3145728 | bytes 10485762 | tf_op jit(solution)/shard_map/reduce_sum | solution.py:117
  311.9 3.2 fusion.13
  318.1 4.6 %divide_subtract_fusion = f32[4096,256]{1,0:T(8,128)} fusion(f32[4096,256]{1,0:T(8,128)S(1)} %copy-done.1, f32[4096]{0:T(1024)S(1)} %get-tuple-element.158, f32[4096]{0:T(1024)S(1)} %add_sqrt_fusion, f32[4096]{0:T(1024)S(1)} %fusion.13, bf16[4096,256]{1,0:T(8,128)(2,1)S(1)} %reduce_sum.92), kind=kLoop, calls=%fused_computation.31 | loop fusion | flops 8388608 | bytes 10534912 | tf_op jit(solution)/shard_map/sub | solution.py:120
  (93 shorter events, 25.6 us)
Async XLA Ops:
  17.1 12.0 %all-to-all-start = ((s32[8,1,384]{2,1,0:T(1,128)}), s32[8,1,384]{2,1,0:T(1,128)S(1)}, u32[]{:S(2)}, u32[]{:S(2)}) async-start(s32[8,1,384]{2,1,0:T(1,128)} %bitcast.5), calls=%async_computation | async-start | bytes 24576 | tf_op jit(solution)/shard_map/all_to_all | solution.py:37
  23.5 3.4 %copy-start = (f32[4096,256]{1,0:T(8,128)S(1)}, f32[4096,256]{1,0:T(8,128)}, u32[]{:S(2)}) copy-start(f32[4096,256]{1,0:T(8,128)} %param.11) | copy-start | bytes 12582916
  42.2 4.5 %copy-start.9 = (u32[32]{0:T(128)S(1)}, u32[32]{0:T(128)}, u32[]{:S(2)}) copy-start(u32[32]{0:T(128)} %constant.31) | copy-start | bytes 388
  42.2 5.8 %copy-start.8 = (s32[48]{0:T(128)S(1)}, s32[48]{0:T(128)}, u32[]{:S(2)}) copy-start(s32[48]{0:T(128)} %param.15) | copy-start | bytes 580
  42.2 79.0 %copy-start.5 = (s32[1024,1]{0,1:T(1,128)S(1)}, s32[1024,1]{0,1:T(1,128)}, u32[]{:S(2)}) copy-start(s32[1024,1]{0,1:T(1,128)} %param.13) | copy-start | bytes 12292
  42.2 79.0 %copy-start.7 = (s32[1024]{0:T(1024)S(1)}, s32[1024]{0:T(1024)}, u32[]{:S(2)}) copy-start(s32[1024]{0:T(1024)} %param.14) | copy-start | bytes 12292
  42.2 79.1 %all-to-all-start.1 = ((bf16[8,384,256]{2,1,0:T(8,128)(2,1)}), bf16[8,384,256]{2,1,0:T(8,128)(2,1)}, u32[]{:S(2)}, u32[]{:S(2)}) async-start(bf16[8,384,256]{2,1,0:T(8,128)(2,1)} %bitcast.98), calls=%async_computation.1 | async-start | bytes 3145728 | tf_op jit(solution)/shard_map/all_to_all | solution.py:39
  107.5 18.9 %copy-start.2 = (bf16[1024,256]{1,0:T(8,128)(2,1)S(1)}, bf16[1024,256]{1,0:T(8,128)(2,1)}, u32[]{:S(2)}) copy-start(bf16[1024,256]{1,0:T(8,128)(2,1)} %param.10) | copy-start | bytes 1572868
  139.7 48.9 %all-to-all-start.2 = ((bf16[8,384,256]{2,1,0:T(8,128)(2,1)}), bf16[8,384,256]{2,1,0:T(8,128)(2,1)}, u32[]{:S(2)}, u32[]{:S(2)}) async-start(bf16[8,384,256]{2,1,0:T(8,128)(2,1)} %bitcast.99), calls=%async_computation.2 | async-start | bytes 3145728 | tf_op jit(solution)/shard_map/all_to_all | solution.py:97
  144.0 67.4 %reduce-scatter.2.cloned.1.call-start = ((), (), s32[]{:S(2)}) async-start(), calls=%async_computation.4 | async-start | bytes 884736 | tf_op jit(solution)/shard_map/reduce_scatter | solution.py:109
  144.1 1.1 copy-start.3
  145.7 0.9 copy-start.4
  146.6 1.1 copy-start.3
  148.1 0.9 copy-start.4
  149.0 1.1 copy-start.3
  150.6 0.9 copy-start.4
  153.6 152.3 %all-gather.6.cloned.1.call-start = ((), (), s32[]{:S(2)}) async-start(), calls=%async_computation.5 | async-start | bytes 10485760 | tf_op jit(solution)/shard_map/all_gather | solution.py:117
  311.9 3.5 %copy-start.1 = (f32[4096,256]{1,0:T(8,128)S(1)}, f32[4096,256]{1,0:T(8,128)}, u32[]{:S(2)}) copy-start(f32[4096,256]{1,0:T(8,128)} %param.11) | copy-start | bytes 12582916
  315.4 2.0 copy-start.6
Sparse Core Ops, SparseCore 0:
  153.7 36.1 reduce-scatter.1
  221.4 84.4 all-gather.5
